TPU v7x, 32 devices: a whole 2x2x4 slice. The times are simulated.
32 devices in a mesh: dp: 8 (over y, x, core), seq: 4 (over z).
Axes of the slice: x: 2, y: 2, z: 4, core: 2. Of those that a mesh axis runs over, the one named last changes fastest.
Arguments:
- hidden: bfloat16 [16, 1024, 768], P('dp', 'seq'), may hold values from -6 to 6
- cotangent: bfloat16 [16, 1024, 768], P('dp', 'seq'), may hold values from -6 to 6
- w_proj: bfloat16 [768, 1920], P(('dp', 'seq')), may hold values from -0.3125 to 0.3125
- w_depth: bfloat16 [768, 9], P(('dp', 'seq')), may hold values from -2 to 2
- w_kernel: bfloat16 [384, 54], replicated, may hold values from -0.3125 to 0.3125
- b_kernel: bfloat16 [54], replicated, may hold values from -3 to 3
- w_out: bfloat16 [768, 768], P(('dp', 'seq')), may hold values from -0.4375 to 0.4375
- w_up: bfloat16 [768, 1536], P(('dp', 'seq')), may hold values from -0.3125 to 0.3125
- w_down: bfloat16 [3072, 384], P(('dp', 'seq')), may hold values from -0.21875 to 0.21875
- b_proj: bfloat16 [1536], P(('dp', 'seq')), may hold values from -3 to 3
- b_up: bfloat16 [3072], P(('dp', 'seq')), may hold values from -3 to 3
- b_out: bfloat16 [768], P(('dp', 'seq')), may hold values from -3 to 3
- ln1_gain: bfloat16 [768], P(('dp', 'seq')), may hold values from 0.5 to 1.5
- ln1_bias: bfloat16 [768], P(('dp', 'seq')), may hold values from -3 to 3
- b_down: bfloat16 [768], P(('dp', 'seq')), may hold values from -3 to 3
- ln2_gain: bfloat16 [768], P(('dp', 'seq')), may hold values from 0.5 to 1.5
- ln2_bias: bfloat16 [768], P(('dp', 'seq')), may hold values from -3 to 3
Outputs:
- output: bfloat16 [16, 1024, 768], P('dp', 'seq')
- grad_hidden: float32 [16, 1024, 768], P('dp', 'seq')
- grad_w_proj: float32 [768, 1920], P(('dp', 'seq'))
- grad_w_depth: float32 [768, 9], P(('dp', 'seq'))
- grad_w_kernel: float32 [384, 54], replicated
- grad_b_kernel: float32 [54], replicated
- grad_w_out: float32 [768, 768], P(('dp', 'seq'))
- grad_w_up: float32 [768, 1536], P(('dp', 'seq'))
- grad_w_down: float32 [3072, 384], P(('dp', 'seq'))
- grad_b_proj: float32 [1536], P(('dp', 'seq'))
- grad_b_up: float32 [3072], P(('dp', 'seq'))
- grad_b_out: float32 [768], P(('dp', 'seq'))
- grad_ln1_gain: float32 [768], P(('dp', 'seq'))
- grad_ln1_bias: float32 [768], P(('dp', 'seq'))
- grad_b_down: float32 [768], P(('dp', 'seq'))
- grad_ln2_gain: float32 [768], P(('dp', 'seq'))
- grad_ln2_bias: float32 [768], P(('dp', 'seq'))
All inputs are finite; a program needn't handle non-finite values.
Results may differ from a plain program's by a relative error of at most 0.014.
The roundings to bfloat16 on the way count: a program that leaves them out, or rounds other values in their place, can miss the bound.
Values may be sent and summed in bfloat16 or wider, within the bound.
A program may use at most 256 MiB of HBM per device.

v0:
```python
from functools import partial

import jax
import jax.numpy as jnp
from jax import lax
from jax.sharding import PartitionSpec as P

HEADS = 6
HEAD = 64
KERNEL = 9
FF = 3072
GROUPS = 2


norm_eps = 1e-12


def with_halo(cells, sides, width):
    for axis, dim in sides:
        count = lax.axis_size(axis)
        ends = count - 1
        head = lax.slice_in_dim(cells, 0, width, axis=dim)
        tail = lax.slice_in_dim(cells, cells.shape[dim] - width, cells.shape[dim], axis=dim)
        cells = jnp.concatenate(
            [
                lax.ppermute(tail, axis, [(i, (i + 1) % count) for i in range(ends)]),
                cells,
                lax.ppermute(head, axis, [((i + 1) % count, i) for i in range(ends)]),
            ],
            axis=dim,
        )
    return cells


def layer_norm(inputs, gain_vec, shift_vec):
    centre = inputs - jnp.mean(inputs, axis=-1, keepdims=True)
    variance = jnp.mean(centre * centre, axis=-1, keepdims=True)
    return centre * lax.rsqrt(variance + norm_eps) * gain_vec + shift_vec


def attend(queries, key_rows, value_rows, score_scale):
    scores = (
        jnp.einsum("ihe,jhe->hij", queries, key_rows, preferred_element_type=jnp.float32)
        * score_scale
    )
    row_max = jnp.max(scores, axis=-1, keepdims=True)
    norm_log = row_max + jnp.log(jnp.sum(jnp.exp(scores - row_max), axis=-1, keepdims=True))
    weights_low = jnp.exp(scores - norm_log).astype(jnp.bfloat16)
    context = jnp.einsum(
        "hij,jhe->ihe", weights_low, value_rows, preferred_element_type=jnp.float32
    )
    return (context.astype(jnp.bfloat16), norm_log[..., 0])


def attend_back(queries, grad_context, norm_log, key_rows, value_rows, row_delta, score_scale):
    scores = (
        jnp.einsum("ihe,jhe->hij", queries, key_rows, preferred_element_type=jnp.float32)
        * score_scale
    )
    soft_rows = jnp.exp(scores - norm_log[..., None])
    grad_soft = jnp.einsum(
        "ihe,jhe->hij", grad_context, value_rows, preferred_element_type=jnp.float32
    )
    row_delta = jnp.sum(soft_rows * grad_soft, axis=-1)
    grad_scores = (soft_rows * (grad_soft - row_delta[..., None])).astype(jnp.bfloat16)
    grad_queries = (
        jnp.einsum("hij,jhe->ihe", grad_scores, key_rows, preferred_element_type=jnp.float32)
        * score_scale
    )
    grad_keys = (
        jnp.einsum("hij,ihe->jhe", grad_scores, queries, preferred_element_type=jnp.float32)
        * score_scale
    )
    grad_values = jnp.einsum(
        "hij,ihe->jhe",
        soft_rows.astype(jnp.bfloat16),
        grad_context,
        preferred_element_type=jnp.float32,
    )
    return (grad_queries, grad_keys, grad_values, row_delta)


def body(
    hidden,
    cotangent,
    w_proj,
    w_depth,
    w_kernel,
    b_kernel,
    w_out,
    w_up,
    w_down,
    b_proj,
    b_up,
    b_out,
    ln1_gain,
    ln1_bias,
    b_down,
    ln2_gain,
    ln2_bias,
):
    seq_count, local_rows, model_width = hidden.shape
    total_rows = seq_count * local_rows
    head_count = HEADS
    head_size = HEAD
    all_width = head_count * head_size
    tap_count = KERNEL
    half_kernel = KERNEL // 2
    group_count = GROUPS
    hidden_units = FF
    ext_rows = local_rows + 2 * half_kernel
    score_scale = head_size ** (-0.5)
    gathered = (
        lax.all_gather(w_proj, ("dp", "seq"), axis=0, tiled=True),
        lax.all_gather(w_depth, ("dp", "seq"), axis=0, tiled=True),
        lax.all_gather(w_out, ("dp", "seq"), axis=0, tiled=True),
        lax.all_gather(w_up, ("dp", "seq"), axis=0, tiled=True),
        lax.all_gather(w_down, ("dp", "seq"), axis=0, tiled=True),
        lax.all_gather(b_proj, ("dp", "seq"), axis=0, tiled=True),
        lax.all_gather(b_up, ("dp", "seq"), axis=0, tiled=True),
        lax.all_gather(b_out, ("dp", "seq"), axis=0, tiled=True),
        lax.all_gather(ln1_gain, ("dp", "seq"), axis=0, tiled=True),
        lax.all_gather(ln1_bias, ("dp", "seq"), axis=0, tiled=True),
        lax.all_gather(b_down, ("dp", "seq"), axis=0, tiled=True),
        lax.all_gather(ln2_gain, ("dp", "seq"), axis=0, tiled=True),
        lax.all_gather(ln2_bias, ("dp", "seq"), axis=0, tiled=True),
    )
    (
        full_proj,
        full_depth,
        full_out,
        full_up,
        full_down,
        full_bproj,
        full_bup,
        full_bout,
        gain_one,
        shift_one,
        full_bdown,
        gain_two,
        shift_two,
    ) = gathered
    bias_proj = full_bproj.astype(jnp.float32)
    gain_first = gain_one.astype(jnp.float32)
    shift_first = shift_one.astype(jnp.float32)
    gain_second = gain_two.astype(jnp.float32)
    shift_second = shift_two.astype(jnp.float32)
    tokens_flat = hidden.reshape(total_rows, model_width)
    first_proj = jnp.dot(
        tokens_flat, full_proj[:, : 3 * all_width], preferred_element_type=jnp.float32
    )
    queries = (first_proj[:, :all_width] + bias_proj[:all_width]).astype(jnp.bfloat16)
    key_rows = first_proj[:, all_width : 2 * all_width].astype(jnp.bfloat16)
    value_rows = (first_proj[:, 2 * all_width :] + bias_proj[all_width : 2 * all_width]).astype(
        jnp.bfloat16
    )
    extended = with_halo(hidden, (("seq", 1),), half_kernel)
    position = lax.axis_index("seq") * local_rows + jnp.arange(ext_rows) - half_kernel
    inside = ((position >= 0) & (position < local_rows * lax.axis_size("seq"))).astype(jnp.float32)
    conv_input = jnp.dot(
        extended.reshape(seq_count * ext_rows, model_width),
        full_proj[:, 3 * all_width : 4 * all_width],
        preferred_element_type=jnp.float32,
    )
    conv_input = (conv_input + bias_proj[2 * all_width : 3 * all_width]).reshape(
        seq_count, ext_rows, all_width
    ) * inside[None, :, None]
    depth_weights = full_depth.astype(jnp.float32)
    depth_sum = jnp.zeros((seq_count, local_rows, model_width), jnp.float32)
    for tap_index in range(tap_count):
        depth_sum = (
            depth_sum
            + extended[:, tap_index : tap_index + local_rows].astype(jnp.float32)
            * depth_weights[:, tap_index]
        )
    spread = depth_sum.astype(jnp.bfloat16).reshape(total_rows, model_width)
    key_conv = (
        jnp.dot(spread, full_proj[:, 4 * all_width :], preferred_element_type=jnp.float32)
        + bias_proj[3 * all_width :]
    )
    mixed_key = (key_conv * queries.astype(jnp.float32)).astype(jnp.bfloat16)
    logits = jnp.dot(mixed_key, w_kernel, preferred_element_type=jnp.float32) + b_kernel.astype(
        jnp.float32
    )
    tap_weights = jax.nn.softmax(
        logits.reshape(seq_count, local_rows, head_count, tap_count), axis=-1
    )
    conv_heads = conv_input.reshape(seq_count, ext_rows, head_count, head_size)
    conv_mix = jnp.zeros((seq_count, local_rows, head_count, head_size), jnp.float32)
    for tap_index in range(tap_count):
        conv_mix = (
            conv_mix
            + tap_weights[..., tap_index, None] * conv_heads[:, tap_index : tap_index + local_rows]
        )
    queries_seq = queries.reshape(seq_count, local_rows, all_width)
    all_keys, all_values = (
        lax.all_gather(
            key_rows.reshape(seq_count, local_rows, all_width), "seq", axis=1, tiled=True
        ),
        lax.all_gather(
            value_rows.reshape(seq_count, local_rows, all_width), "seq", axis=1, tiled=True
        ),
    )
    full_length = all_keys.shape[1]

    def forward_one(item_set):
        query_seq, key_seq, value_seq = item_set
        return attend(
            query_seq.reshape(local_rows, head_count, head_size),
            key_seq.reshape(full_length, head_count, head_size),
            value_seq.reshape(full_length, head_count, head_size),
            score_scale,
        )

    context, norm_log = lax.map(forward_one, (queries_seq, all_keys, all_values))
    joined = jnp.concatenate(
        [
            context.reshape(total_rows, all_width),
            conv_mix.reshape(total_rows, all_width).astype(jnp.bfloat16),
        ],
        axis=-1,
    )
    after_mix = (
        jnp.dot(joined, full_out, preferred_element_type=jnp.float32)
        + full_bout.astype(jnp.float32)
        + tokens_flat.astype(jnp.float32)
    )
    first_norm, first_pull = jax.vjp(layer_norm, after_mix, gain_first, shift_first)
    grouped_in = first_norm.astype(jnp.bfloat16).reshape(
        total_rows, group_count, model_width // group_count
    )
    up_groups = full_up.reshape(
        group_count, model_width // group_count, hidden_units // group_count
    )
    pre_act = jnp.einsum(
        "ngd,gdf->ngf", grouped_in, up_groups, preferred_element_type=jnp.float32
    ).reshape(total_rows, hidden_units) + full_bup.astype(jnp.float32)
    activated, gelu_pull = jax.vjp(partial(jax.nn.gelu, approximate=False), pre_act)
    act_low = activated.astype(jnp.bfloat16).reshape(
        total_rows, group_count, hidden_units // group_count
    )
    down_groups = full_down.reshape(
        group_count, hidden_units // group_count, model_width // group_count
    )
    summed = jnp.einsum(
        "ngf,gfd->ngd", act_low, down_groups, preferred_element_type=jnp.float32
    ).reshape(total_rows, model_width)
    summed = summed + full_bdown.astype(jnp.float32) + first_norm
    out_value, second_pull = jax.vjp(layer_norm, summed, gain_second, shift_second)
    output = out_value.astype(jnp.bfloat16).reshape(seq_count, local_rows, model_width)
    back_set = (
        lax.all_gather(w_proj, ("dp", "seq"), axis=0, tiled=True),
        lax.all_gather(w_depth, ("dp", "seq"), axis=0, tiled=True),
        lax.all_gather(w_out, ("dp", "seq"), axis=0, tiled=True),
        lax.all_gather(w_up, ("dp", "seq"), axis=0, tiled=True),
        lax.all_gather(w_down, ("dp", "seq"), axis=0, tiled=True),
        lax.all_gather(b_proj, ("dp", "seq"), axis=0, tiled=True),
        lax.all_gather(b_up, ("dp", "seq"), axis=0, tiled=True),
        lax.all_gather(b_out, ("dp", "seq"), axis=0, tiled=True),
        lax.all_gather(ln1_gain, ("dp", "seq"), axis=0, tiled=True),
        lax.all_gather(ln1_bias, ("dp", "seq"), axis=0, tiled=True),
        lax.all_gather(b_down, ("dp", "seq"), axis=0, tiled=True),
        lax.all_gather(ln2_gain, ("dp", "seq"), axis=0, tiled=True),
        lax.all_gather(ln2_bias, ("dp", "seq"), axis=0, tiled=True),
    )
    back_proj = back_set[0]
    back_depth = back_set[1].astype(jnp.float32)
    back_out = back_set[2]
    back_up = back_set[3].reshape(
        group_count, model_width // group_count, hidden_units // group_count
    )
    back_down = back_set[4].reshape(
        group_count, hidden_units // group_count, model_width // group_count
    )
    grad_summed, grad_gain_two, grad_shift_two = second_pull(
        cotangent.reshape(total_rows, model_width).astype(jnp.float32)
    )
    grad_bdown = jnp.sum(grad_summed, axis=0)
    summed_low = grad_summed.astype(jnp.bfloat16).reshape(
        total_rows, group_count, model_width // group_count
    )
    grad_activ = jnp.einsum(
        "ngd,gfd->ngf", summed_low, back_down, preferred_element_type=jnp.float32
    ).reshape(total_rows, hidden_units)
    grad_wdown = jnp.einsum(
        "ngf,ngd->gfd", act_low, summed_low, preferred_element_type=jnp.float32
    ).reshape(hidden_units, model_width // group_count)
    grad_pre = gelu_pull(grad_activ)[0]
    grad_bup = jnp.sum(grad_pre, axis=0)
    pre_low = grad_pre.astype(jnp.bfloat16).reshape(
        total_rows, group_count, hidden_units // group_count
    )
    grad_wup = jnp.einsum(
        "ngd,ngf->gdf", grouped_in, pre_low, preferred_element_type=jnp.float32
    ).reshape(model_width, hidden_units // group_count)
    grad_first = grad_summed + jnp.einsum(
        "ngf,gdf->ngd", pre_low, back_up, preferred_element_type=jnp.float32
    ).reshape(total_rows, model_width)
    grad_after, grad_gain_one, grad_shift_one = first_pull(grad_first)
    grad_bout = jnp.sum(grad_after, axis=0)
    after_low = grad_after.astype(jnp.bfloat16)
    grad_wout = jnp.dot(joined.T, after_low, preferred_element_type=jnp.float32)
    grad_joined = jnp.dot(after_low, back_out.T, preferred_element_type=jnp.float32)
    grad_context = (
        grad_joined[:, :all_width].astype(jnp.bfloat16).reshape(seq_count, local_rows, all_width)
    )
    grad_mix = grad_joined[:, all_width:].reshape(seq_count, local_rows, head_count, head_size)

    def back_one(item_set):
        query_seq, grad_seq, norm_seq, key_seq, value_seq = item_set
        grad_query, grad_key, grad_value, unused_delta = attend_back(
            query_seq.reshape(local_rows, head_count, head_size),
            grad_seq.reshape(local_rows, head_count, head_size),
            norm_seq,
            key_seq.reshape(full_length, head_count, head_size),
            value_seq.reshape(full_length, head_count, head_size),
            None,
            score_scale,
        )
        key_value = jnp.concatenate(
            [grad_key.reshape(full_length, all_width), grad_value.reshape(full_length, all_width)],
            axis=-1,
        )
        return (grad_query.reshape(local_rows, all_width), key_value)

    grad_query_att, kv_terms = lax.map(
        back_one, (queries_seq, grad_context, norm_log, all_keys, all_values)
    )
    own_kv = lax.psum_scatter(
        kv_terms.astype(jnp.bfloat16), "seq", scatter_dimension=1, tiled=True
    ).astype(jnp.float32)
    grad_keys_low = own_kv[..., :all_width].reshape(total_rows, all_width).astype(jnp.bfloat16)
    grad_values_low = own_kv[..., all_width:].reshape(total_rows, all_width).astype(jnp.bfloat16)
    grad_taps = jnp.stack(
        [
            jnp.sum(grad_mix * conv_heads[:, tap_index : tap_index + local_rows], axis=-1)
            for tap_index in range(tap_count)
        ],
        axis=-1,
    )
    grad_conv_ext = jnp.zeros((seq_count, ext_rows, head_count, head_size), jnp.float32)
    for tap_index in range(tap_count):
        grad_conv_ext = grad_conv_ext + jnp.pad(
            tap_weights[..., tap_index, None] * grad_mix,
            ((0, 0), (tap_index, 2 * half_kernel - tap_index), (0, 0), (0, 0)),
        )
    grad_logits = tap_weights * (
        grad_taps - jnp.sum(tap_weights * grad_taps, axis=-1, keepdims=True)
    )
    grad_logits = grad_logits.reshape(total_rows, head_count * tap_count)
    grad_bkernel = jnp.sum(grad_logits, axis=0)
    logits_low = grad_logits.astype(jnp.bfloat16)
    grad_wkernel = jnp.dot(mixed_key.T, logits_low, preferred_element_type=jnp.float32)
    grad_mixed = jnp.dot(logits_low, w_kernel.T, preferred_element_type=jnp.float32)
    grad_queries = (grad_query_att.reshape(total_rows, all_width) + grad_mixed * key_conv).astype(
        jnp.bfloat16
    )
    grad_key_conv = grad_mixed * queries.astype(jnp.float32)
    grad_bpt = jnp.sum(grad_key_conv, axis=0)
    key_conv_low = grad_key_conv.astype(jnp.bfloat16)
    grad_wpt = jnp.dot(spread.T, key_conv_low, preferred_element_type=jnp.float32)
    grad_spread = jnp.dot(
        key_conv_low, back_proj[:, 4 * all_width :].T, preferred_element_type=jnp.float32
    ).reshape(seq_count, local_rows, model_width)
    grad_wdepth = jnp.stack(
        [
            jnp.sum(
                extended[:, tap_index : tap_index + local_rows].astype(jnp.float32) * grad_spread,
                axis=(0, 1),
            )
            for tap_index in range(tap_count)
        ],
        axis=-1,
    )
    grad_ext_depth = jnp.zeros((seq_count, ext_rows, model_width), jnp.float32)
    for tap_index in range(tap_count):
        grad_ext_depth = grad_ext_depth + jnp.pad(
            back_depth[:, tap_index] * grad_spread,
            ((0, 0), (tap_index, 2 * half_kernel - tap_index), (0, 0)),
        )
    combined = jnp.concatenate(
        [grad_conv_ext.reshape(seq_count, ext_rows, all_width), grad_ext_depth], axis=-1
    )
    received = with_halo(combined.astype(jnp.bfloat16), (("seq", 1),), half_kernel).astype(
        combined.dtype
    )
    own_part = combined[:, half_kernel : half_kernel + local_rows]
    own_part = own_part.at[:, :half_kernel].add(received[:, :half_kernel])
    own_part = own_part.at[:, local_rows - half_kernel :].add(
        received[:, received.shape[1] - half_kernel :]
    )
    grad_conv_own = own_part[..., :all_width].reshape(total_rows, all_width)
    grad_depth_x = own_part[..., all_width:].reshape(total_rows, model_width)
    grad_bconv = jnp.sum(grad_conv_own, axis=0)
    conv_low = grad_conv_own.astype(jnp.bfloat16)
    stacked = jnp.concatenate([grad_queries, grad_keys_low, grad_values_low, conv_low], axis=-1)
    grad_wfirst = jnp.dot(tokens_flat.T, stacked, preferred_element_type=jnp.float32)
    grad_tokens = (
        grad_after
        + jnp.dot(stacked, back_proj[:, : 4 * all_width].T, preferred_element_type=jnp.float32)
        + grad_depth_x
    )
    grad_wproj = jnp.concatenate([grad_wfirst, grad_wpt], axis=1)
    grad_bproj = jnp.concatenate(
        [
            jnp.sum(grad_queries.astype(jnp.float32), axis=0),
            jnp.sum(grad_values_low.astype(jnp.float32), axis=0),
            grad_bconv,
            grad_bpt,
        ]
    )
    shards = (
        lax.psum_scatter(grad_wproj, ("dp", "seq"), scatter_dimension=0, tiled=True),
        lax.psum_scatter(grad_wdepth, ("dp", "seq"), scatter_dimension=0, tiled=True),
        lax.psum_scatter(grad_wout, ("dp", "seq"), scatter_dimension=0, tiled=True),
        lax.psum_scatter(grad_wup, ("dp", "seq"), scatter_dimension=0, tiled=True),
        lax.psum_scatter(grad_wdown, ("dp", "seq"), scatter_dimension=0, tiled=True),
        lax.psum_scatter(grad_bproj, ("dp", "seq"), scatter_dimension=0, tiled=True),
        lax.psum_scatter(grad_bup, ("dp", "seq"), scatter_dimension=0, tiled=True),
        lax.psum_scatter(grad_bout, ("dp", "seq"), scatter_dimension=0, tiled=True),
        lax.psum_scatter(grad_gain_one, ("dp", "seq"), scatter_dimension=0, tiled=True),
        lax.psum_scatter(grad_shift_one, ("dp", "seq"), scatter_dimension=0, tiled=True),
        lax.psum_scatter(grad_bdown, ("dp", "seq"), scatter_dimension=0, tiled=True),
        lax.psum_scatter(grad_gain_two, ("dp", "seq"), scatter_dimension=0, tiled=True),
        lax.psum_scatter(grad_shift_two, ("dp", "seq"), scatter_dimension=0, tiled=True),
    )
    kernel_total = lax.psum((grad_wkernel, grad_bkernel), ("dp", "seq"))
    return (
        output,
        grad_tokens.reshape(seq_count, local_rows, model_width),
        shards[0],
        shards[1],
        kernel_total[0],
        kernel_total[1],
        shards[2],
        shards[3],
        shards[4],
        shards[5],
        shards[6],
        shards[7],
        shards[8],
        shards[9],
        shards[10],
        shards[11],
        shards[12],
    )


def solution(mesh):
    placed = (
        P("dp", "seq", None),
        P("dp", "seq", None),
        P(("dp", "seq"), None),
        P(("dp", "seq"), None),
        P(),
        P(),
        P(("dp", "seq"), None),
        P(("dp", "seq"), None),
        P(("dp", "seq"), None),
        P(("dp", "seq")),
        P(("dp", "seq")),
        P(("dp", "seq")),
        P(("dp", "seq")),
        P(("dp", "seq")),
        P(("dp", "seq")),
        P(("dp", "seq")),
        P(("dp", "seq")),
    )
    return jax.shard_map(
        body,
        mesh=mesh,
        in_specs=placed,
        out_specs=(
            P("dp", "seq", None),
            P("dp", "seq", None),
            P(("dp", "seq"), None),
            P(("dp", "seq"), None),
            P(),
            P(),
            P(("dp", "seq"), None),
            P(("dp", "seq"), None),
            P(("dp", "seq"), None),
            P(("dp", "seq")),
            P(("dp", "seq")),
            P(("dp", "seq")),
            P(("dp", "seq")),
            P(("dp", "seq")),
            P(("dp", "seq")),
            P(("dp", "seq")),
            P(("dp", "seq")),
        ),
        check_vma=False,
    )
```

profile of v0, /device:TPU:0, one launch (start us, length us, event | category | flops | bytes accessed | tf_op | source)
XLA Modules:
  0.0 980.3 jit_solution(8224273836955006827)
XLA Ops:
  14.7 42.5 %all-reduce.38 = (bf16[1536]{0:T(1024)(128)(2,1)S(1)}, bf16[3072]{0:T(1024)(128)(2,1)S(1)}, bf16[768]{0:T(1024)(128)(2,1)S(1)}, bf16[768]{0:T(1024)(128)(2,1)S(1...) all-reduce(bf16[1536]{0:T(1024)(128)(2,1)S(1)} %dynamic-update-slic, ...), channel_id=1, replica_groups=mesh['dp'=8,'seq'=4] {'dp','seq'}, use_global_device_ids=true, to_apply=%add.18 | all-reduce | flops 9216 | bytes 36864
  57.2 15.2 %all-gather.8.cloned.1.call-done = bf16[768,1920]{1,0:T(8,128)(2,1)} async-done(((bf16[24,1920]{1,0:T(8,128)(2,1)}), bf16[768,1920]{1,0:T(8,128)(2,1)}) %all-gather.8.cloned.1.call-update) | async-done | bytes 2949136 | tf_op jit(solution)/shard_map/all_gather | solution.py:114
  82.5 4.5 collective-permute-start
  87.2 66.9 %all-gather = bf16[32,24,9]{1,2,0:T(8,128)(2,1)S(1)} all-gather(bf16[1,24,9]{1,2,0:T(8,128)(2,1)S(1)} %bitcast.392), channel_id=1, replica_groups=mesh['dp'=8,'seq'=4] {'dp','seq'}, dimensions={0}, use_global_device_ids=true | all-gather | bytes 14256 | tf_op jit(solution)/shard_map/all_gather | solution.py:115
  165.0 6.7 add_convert_fusion.3
  173.5 10.9 %while.26 = (s32[]{:T(128)}, bf16[2,256,6,64]{1,3,2,0:T(8,128)(2,1)S(1)}, f32[2,6,256]{2,1,0:T(8,128)S(1)}, bf16[2,1024,384]{1,2,0:T(8,128)(2,1)}, bf16[2,256,38...) while((s32[]{:T(128)}, bf16[2,256,6,64]{1,3,2,0:T(8,128)(2,1)S(1)}, ...), condition=%wide.region_3.4_spmd, body=%wide.region_0.3_spmd.sunk | while | flops 415332864 | bytes 24438876 | solution.py:215
  185.9 24.1 %all-gather.14.cloned.1.call-done = bf16[768,768]{1,0:T(8,128)(2,1)} async-done(((bf16[24,768]{1,0:T(8,128)(2,1)}), bf16[768,768]{1,0:T(8,128)(2,1)}) %all-gather.14.cloned.1.call-update) | async-done | bytes 1179664 | tf_op jit(solution)/shard_map/all_gather | solution.py:116
  216.5 52.4 %all-gather.16.cloned.1.call-done = bf16[768,1536]{1,0:T(8,128)(2,1)} async-done(((bf16[24,1536]{1,0:T(8,128)(2,1)}), bf16[768,1536]{1,0:T(8,128)(2,1)}) %all-gather.16.cloned.1.call-update) | async-done | bytes 2359312 | tf_op jit(solution)/shard_map/all_gather | solution.py:117
  269.0 18.5 %fusion.22 = (bf16[512,2,1536]{2,0,1:T(8,128)(2,1)}, f32[512,2,1536]{2,0,1:T(8,128)}, f32[2,512,1536]{2,1,0:T(8,128)}) fusion(f32[2,1536]{1,0:T(2,128)S(1)} %reshape.392, bf16[512,2,384]{0,2,1:T(8,128)(2,1)} %bitcast.360, bf16[2,384,1536]{2,1,0:T(8,128)(2,1)} %bitcast.393), kind=kOutput, calls=%fused_computation.49 | convolution fusion | flops 1311768576 | bytes 18886656 | tf_op jit(solution)/shard_map/ngd,gdf->ngf/dot_general | solution.py:235
  287.5 40.4 %all-gather.18.cloned.1.call-done = bf16[3072,384]{1,0:T(8,128)(2,1)} async-done(((bf16[96,384]{1,0:T(8,128)(2,1)}), bf16[3072,384]{1,0:T(8,128)(2,1)}) %all-gather.18.cloned.1.call-update) | async-done | bytes 2359312 | tf_op jit(solution)/shard_map/all_gather | solution.py:118
  327.9 5.2 fusion.126
  345.0 6.4 fusion.124
  364.8 9.0 multiply_reduce_fusion.6
  373.8 10.0 %pad_add_fusion.1 = f32[2,264,6,64]{1,0,3,2:T(2,128)S(1)} fusion(f32[2,256,6,64]{1,0,3,2:T(2,128)S(1)} %get-tuple-element.380, f32[2,256,6,64]{1,0,3,2:T(2,128)S(1)} %get-tuple-element.379, f32[2,256,6,64]{1,0,3,2:T(2,128)S(1)} %get-tuple-element.378, f32[2,256,6,64]{1,0,3,2:T(2,128)S(1)} %get-tuple-element.377, ...), kind=kLoop, calls=%fused_computation.147 | loop fusion | flops 1622016 | bytes 7888896 | tf_op jit(solution)/shard_map/add | solution.py:343
  385.7 34.7 %while.27 = (s32[]{:T(128)}, f32[2,256,384]{2,1,0:T(8,128)}, bf16[2,1024,768]{1,2,0:T(8,128)(2,1)}, bf16[2,1024,384]{1,2,0:T(8,128)(2,1)}, bf16[2,256,384]{1,2,0...) while((s32[]{:T(128)}, f32[2,256,384]{2,1,0:T(8,128)}, ...), condition=%wide.region_16.17_spmd, body=%wide.region_14.16_spmd.sunk | while | flops 1029536256 | bytes 111716632 | solution.py:326
  444.0 36.2 %reduce-scatter.7.cloned.1.call-done = bf16[2,256,768]{1,2,0:T(8,128)(2,1)} async-done(((bf16[2,1024,768]{1,2,0:T(8,128)(2,1)}), bf16[2,256,768]{1,2,0:T(8,128)(2,1)}) %reduce-scatter.7.cloned.1.call-update) | async-done | bytes 786448 | tf_op jit(solution)/shard_map/reduce_scatter | solution.py:329
  493.3 6.4 fusion.74
  500.8 5.5 fusion.63
  511.1 42.6 %all-reduce.36 = (f32[768,9]{0,1:T(8,128)S(1)}, f32[54]{0:T(128)}, f32[1536]{0:T(1024)S(1)}, f32[3072]{0:T(1024)S(1)}, f32[768]{0:T(1024)S(1)}, /*index=5*/f32[7...) all-reduce(f32[768,9]{0,1:T(8,128)S(1)} %stack.79, ...), channel_id=4, replica_groups=mesh['dp'=8,'seq'=4] {'dp','seq'}, use_global_device_ids=true, to_apply=%region_38.39.clone | all-reduce | flops 16182 | bytes 129456
  559.1 4.8 bitcast_add_fusion
  563.9 78.4 %all-reduce.41.cloned.1.call-done = (f32[768,1920]{0,1:T(8,128)}, f32[384,54]{0,1:T(8,128)}) async-done(((f32[768,1920]{0,1:T(8,128)}, f32[384,54]{0,1:T(8,128)}), (f32[768,1920]{0,1:T(8,128)}, f32[384,54]{0,1:T(8,128)})) %all-reduce.41.cloned.1.call-update) | async-done | bytes 5981200
  645.2 102.4 %reduce-scatter.9.cloned.1.call-done = f32[24,768]{1,0:T(8,128)} async-done(((f32[768,768]{1,0:T(8,128)}), f32[24,768]{1,0:T(8,128)}) %reduce-scatter.9.cloned.1.call-update) | async-done | bytes 73744 | tf_op jit(solution)/shard_map/reduce_scatter | solution.py:415
  747.7 112.0 %reduce-scatter.13.cloned.1.call-done = f32[96,384]{1,0:T(8,128)} async-done(((f32[3072,384]{1,0:T(8,128)}), f32[96,384]{1,0:T(8,128)}) %reduce-scatter.13.cloned.1.call-update) | async-done | bytes 147472 | tf_op jit(solution)/shard_map/reduce_scatter | solution.py:417
  859.6 113.1 %reduce-scatter.11.cloned.1.call-done = f32[24,1536]{1,0:T(8,128)} async-done(((f32[768,1536]{1,0:T(8,128)}), f32[24,1536]{1,0:T(8,128)}) %reduce-scatter.11.cloned.1.call-update) | async-done | bytes 147472 | tf_op jit(solution)/shard_map/reduce_scatter | solution.py:416
  (387 shorter events, 160.3 us)
Async XLA Ops:
  7.2 153.4 %copy-start = (bf16[384,54]{0,1:T(8,128)(2,1)S(1)}, bf16[384,54]{0,1:T(8,128)(2,1)}, u32[]{:S(2)}) copy-start(bf16[384,54]{0,1:T(8,128)(2,1)} %param.29) | copy-start | bytes 124420
  7.2 65.2 %all-gather.8.cloned.1.call-start = ((), (), s32[]{:S(2)}) async-start(), calls=%async_computation.4 | async-start | bytes 3041280 | tf_op jit(solution)/shard_map/all_gather | solution.py:114
  7.9 165.5 %all-gather.10.cloned.1.call-start = ((), (), s32[]{:S(2)}) async-start(), calls=%async_computation.5 | async-start | bytes 1966080 | tf_op jit(solution)/shard_map/all_gather | solution.py:200
  75.5 96.3 %copy-start.3 = (bf16[512,384]{1,0:T(8,128)(2,1)}, bf16[512,384]{1,0:T(8,128)(2,1)S(1)}, u32[]{:S(2)}) copy-start(bf16[512,384]{1,0:T(8,128)(2,1)S(1)} %get-tuple-element.353) | copy-start | bytes 1179652
  77.7 95.7 %all-gather.12.cloned.1.call-start = ((), (), s32[]{:S(2)}) async-start(), calls=%async_computation.6 | async-start | bytes 1966080 | tf_op jit(solution)/shard_map/all_gather | solution.py:197
  79.0 8.2 copy-start.65
  79.9 74.8 %copy-start.69 = (bf16[54]{0:T(256)(128)(2,1)S(1)}, bf16[54]{0:T(256)(128)(2,1)}, u32[]{:S(2)}) copy-start(bf16[54]{0:T(256)(128)(2,1)} %param.30) | copy-start | bytes 328
  80.0 130.1 %all-gather.14.cloned.1.call-start = ((), (), s32[]{:S(2)}) async-start(), calls=%async_computation.7 | async-start | bytes 1216512 | tf_op jit(solution)/shard_map/all_gather | solution.py:116
  80.5 188.4 %all-gather.16.cloned.1.call-start = ((), (), s32[]{:S(2)}) async-start(), calls=%async_computation.8 | async-start | bytes 2433024 | tf_op jit(solution)/shard_map/all_gather | solution.py:117
  81.1 246.8 %all-gather.18.cloned.1.call-start = ((), (), s32[]{:S(2)}) async-start(), calls=%async_computation.9 | async-start | bytes 2433024 | tf_op jit(solution)/shard_map/all_gather | solution.py:118
  81.2 73.6 %collective-permute-start.1 = (bf16[2,4,768]{2,1,0:T(4,128)(2,1)S(1)}, bf16[2,4,768]{2,1,0:T(4,128)(2,1)S(1)}, u32[]{:S(2)}, u32[]{:S(2)}) collective-permute-start(bf16[2,4,768]{2,1,0:T(4,128)(2,1)S(1)} %get-tuple-element.382), channel_id=1, source_target_pairs={{1,0},{2,1},{3,2},{5,4},{6,5},{7,6},{9,8},{10,9},{11,10},{13,12},{... | collective-permute-start | bytes 36872 | tf_op jit(solution)/shard_map/ppermute | solution.py:28
  82.5 72.4 %collective-permute-start = (bf16[2,4,768]{2,1,0:T(4,128)(2,1)S(1)}, bf16[2,4,768]{2,1,0:T(4,128)(2,1)S(1)}, u32[]{:S(2)}, u32[]{:S(2)}) collective-permute-start(bf16[2,4,768]{2,1,0:T(4,128)(2,1)S(1)} %get-tuple-element.381), channel_id=1, source_target_pairs={{0,1},{1,2},{2,3},{4,5},{5,6},{6,7},{8,9},{9,10},{10,11},{12,13},{... | collective-permute-start | bytes 36872 | tf_op jit(solution)/shard_map/ppermute | solution.py:26
  87.1 393.1 %reduce-scatter.7.cloned.1.call-start = ((), (), s32[]{:S(2)}) async-start(), calls=%async_computation.10 | async-start | bytes 3932160 | tf_op jit(solution)/shard_map/reduce_scatter | solution.py:329
  161.1 11.6 %copy-start.38 = (f32[2,256,6]{1,0,2:T(2,128)}, f32[2,256,6]{1,0,2:T(2,128)S(1)}, u32[]{:S(2)}) copy-start(f32[2,256,6]{1,0,2:T(2,128)S(1)} %reduce_max.18) | copy-start | bytes 36868
  161.2 10.8 %copy-start.40 = (f32[2,256,6]{1,0,2:T(2,128)}, f32[2,256,6]{1,0,2:T(2,128)S(1)}, u32[]{:S(2)}) copy-start(f32[2,256,6]{1,0,2:T(2,128)S(1)} %fusion.89) | copy-start | bytes 36868
  345.0 6.4 copy-start.66
  420.5 221.8 %all-reduce.41.cloned.1.call-start = ((), (), s32[]{:S(2)}) async-start(), calls=%async_computation.14 | async-start | bytes 11968512
  430.4 7.0 collective-permute-start.2
  432.8 7.8 collective-permute-start.3
  444.0 38.6 %copy-start.35 = (bf16[2,256,384]{2,1,0:T(8,128)(2,1)}, bf16[2,256,384]{2,1,0:T(8,128)(2,1)S(1)}, u32[]{:S(2)}) copy-start(bf16[2,256,384]{2,1,0:T(8,128)(2,1)S(1)} %slice.524) | copy-start | bytes 1179652
  488.2 259.4 %reduce-scatter.9.cloned.1.call-start = ((), (), s32[]{:S(2)}) async-start(), calls=%async_computation.11 | async-start | bytes 2433024 | tf_op jit(solution)/shard_map/reduce_scatter | solution.py:415
  492.2 367.5 %reduce-scatter.13.cloned.1.call-start = ((), (), s32[]{:S(2)}) async-start(), calls=%async_computation.13 | async-start | bytes 4866048 | tf_op jit(solution)/shard_map/reduce_scatter | solution.py:417
  499.7 473.0 %reduce-scatter.11.cloned.1.call-start = ((), (), s32[]{:S(2)}) async-start(), calls=%async_computation.12 | async-start | bytes 4866048 | tf_op jit(solution)/shard_map/reduce_scatter | solution.py:416
  642.3 330.4 %copy-start.42 = (f32[384,54]{0,1:T(8,128)S(1)}, f32[384,54]{0,1:T(8,128)}, u32[]{:S(2)}) copy-start(f32[384,54]{0,1:T(8,128)} %get-tuple-element.565) | copy-start | bytes 248836
  (70 other events, 162.3 us)
Sparse Core Ops, SparseCore 0:
  10.9 61.5 all-gather.7
  77.8 39.6 all-gather.9
  119.1 34.9 all-gather.11
  156.8 53.2 all-gather.13
  212.7 56.2 all-gather.15
  271.6 56.2 all-gather.17
  420.6 59.5 reduce-scatter.6
  488.4 153.9 all-reduce.40
  649.0 98.5 reduce-scatter.8
  753.6 106.0 reduce-scatter.12
  866.6 106.0 reduce-scatter.10
where the time goes:
time: 986 us; the launch traced here: 980 us
  waiting for transfers between devices  580 us (59%)
  blocking collectives  152 us (15%)
  matrix products  97.8 us (10%)
  local copies, waits for them, and re-layouts  64.8 us (7%)
  other arithmetic  59.3 us (6%)
  between operations  15.7 us (2%)
  starting transfers between devices  10.3 us (1%)
    reduce_scatter x1, waiting for transfers between devices, body(): lax.psum_scatter(grad_wup, ('dp', 'seq'), scatter_dimension=0, tiled=True)  113 us
    reduce_scatter x1, waiting for transfers between devices, body(): lax.psum_scatter(grad_wdown, ('dp', 'seq'), scatter_dimension=0, tiled=True)  112 us
    reduce_scatter x1, waiting for transfers between devices, body(): lax.psum_scatter(grad_wout, ('dp', 'seq'), scatter_dimension=0, tiled=True)  102 us
    unnamed x2, blocking collectives  85.1 us
    unnamed x12, waiting for transfers between devices  80.3 us
    all_gather x1, blocking collectives, body(): lax.all_gather(w_depth, ('dp', 'seq'), axis=0, tiled=True)  66.9 us
    all_gather x1, waiting for transfers between devices, body(): lax.all_gather(w_up, ('dp', 'seq'), axis=0, tiled=True)  52.4 us
    all_gather x1, waiting for transfers between devices, body(): lax.all_gather(w_down, ('dp', 'seq'), axis=0, tiled=True)  40.4 us
  transfers between devices with their start and end apart: 15, of which 10 were waited for; matrix products, arithmetic and copies ran while one was open for 11% of the time, Pallas kernels for 0%

commit v1 on v0

--- a/solution.py
+++ b/solution.py
@@ -3,7 +3,422 @@
 import jax
 import jax.numpy as jnp
 from jax import lax
+from jax.experimental import pallas as pl
+from jax.experimental.pallas import tpu as pltpu
 from jax.sharding import PartitionSpec as P
+
+MESH = pl.DeviceIdType.MESH
+
+
+class Grid:
+    def __init__(self, dp, seq):
+        self.C = 2 if dp % 2 == 0 else 1
+        rest = dp // self.C
+        y = 1
+        while (2 * y) * (2 * y) <= rest and rest % (2 * y) == 0:
+            y *= 2
+        self.Y, self.X, self.Z = y, rest // y, seq
+        d = lax.axis_index("dp")
+        self.z = lax.axis_index("seq")
+        self.c = d % self.C
+        self.x = (d // self.C) % self.X
+        self.y = d // (self.C * self.X)
+        self.dp = d
+    def size(self, ax):
+        return getattr(self, ax.upper())
+    def at(self, **off):
+        g = {a: (getattr(self, a) + off.get(a, 0)) % self.size(a) if off.get(a, 0) else getattr(self, a) for a in "yxcz"}
+        return g
+    def dpof(self, g):
+        return (g["y"] * self.X + g["x"]) * self.C + g["c"]
+    def dev(self, **off):
+        g = self.at(**off)
+        return (self.dpof(g), g["z"])
+
+
+def peers(grid):
+    out = []
+    for a in "zxyc":
+        for o in range(1, grid.size(a)):
+            out.append(grid.dev(**{a: o}))
+    return out
+
+
+def entry_barrier(grid):
+    b = pltpu.get_barrier_semaphore()
+    ps = peers(grid)
+    for p in ps:
+        pl.semaphore_signal(b, inc=1, device_id=p, device_id_type=MESH)
+    pl.semaphore_wait(b, len(ps))
+
+
+class Gather:
+    def __init__(self, grid, src, buf, order, ssem, rsem, lsem):
+        self.g, self.src, self.buf, self.ssem, self.rsem, self.lsem = grid, src, buf, ssem, rsem, lsem
+        self.u, self.v = order[1], order[2]
+        self.ns = 0
+        self.sent = []
+        self.recv = {}
+        g = grid
+        k = 0
+        self.slot = {}
+        for o in range(1, g.Z):
+            self.slot["z", o] = k; k += 1
+        for o in range(1, g.size(self.u)):
+            self.slot["u", o] = k; k += 1
+        for o in range(1, g.size(self.v)):
+            for q in range(g.size(self.u)):
+                self.slot["v", o, q] = k; k += 1
+        for o in range(1, g.C):
+            for q in range(g.size(self.u)):
+                for w in range(g.size(self.v)):
+                    self.slot["c", o, q, w] = k; k += 1
+        self.count = k
+
+    @staticmethod
+    def slots(Z, X, Y, C):
+        return (Z - 1) + X * Y * C - 1
+
+    def block(self, uo, vo, co=0):
+        g = self.g.at(**{self.u: uo, self.v: vo, "c": co})
+        return self.buf.at[pl.ds(self.g.dpof(g) * self.g.Z, self.g.Z)]
+
+    def _send(self, src, dst, slot, dev):
+        k = self.slot[slot]
+        cp = pltpu.make_async_remote_copy(src_ref=src, dst_ref=dst, send_sem=self.ssem.at[k], recv_sem=self.rsem.at[k],
+                                          device_id=dev, device_id_type=MESH)
+        cp.start()
+        self.sent.append(cp)
+
+    def start(self):
+        g = self.g
+        me = g.dp * g.Z + g.z
+        self.local = pltpu.make_async_copy(self.src, self.buf.at[me], self.lsem)
+        self.local.start()
+        for o in range(1, g.Z):
+            self._send(self.src, self.buf.at[me], ("z", o), g.dev(z=o))
+
+    def _wait_recv(self, ref, slot):
+        k = self.slot[slot]
+        pltpu.make_async_remote_copy(src_ref=ref, dst_ref=ref, send_sem=self.ssem.at[k], recv_sem=self.rsem.at[k],
+                                     device_id=self.g.dev(z=1) if self.g.Z > 1 else self.g.dev(c=1), device_id_type=MESH).wait_recv()
+
+    def step1(self):
+        g = self.g
+        self.local.wait()
+        for o in range(1, g.Z):
+            self._wait_recv(self.buf.at[g.dp * g.Z + (g.z + g.Z - o) % g.Z], ("z", o))
+        blk = self.block(0, 0)
+        for o in range(1, g.size(self.u)):
+            self._send(blk, blk, ("u", o), g.dev(**{self.u: o}))
+        for o in range(1, g.size(self.v)):
+            self._send(blk, blk, ("v", o, 0), g.dev(**{self.v: o}))
+        for o in range(1, g.C):
+            self._send(blk, blk, ("c", o, 0, 0), g.dev(c=o))
+
+    def step2(self):
+        g = self.g
+        U, V = g.size(self.u), g.size(self.v)
+        for q in range(1, U):
+            blk = self.block(U - q, 0)
+            self._wait_recv(blk, ("u", q))
+            for o in range(1, V):
+                self._send(blk, blk, ("v", o, q), g.dev(**{self.v: o}))
+            for o in range(1, g.C):
+                self._send(blk, blk, ("c", o, q, 0), g.dev(c=o))
+
+    def step3(self):
+        g = self.g
+        U, V = g.size(self.u), g.size(self.v)
+        for q in range(U):
+            for w in range(1, V):
+                blk = self.block((U - q) % U, V - w)
+                self._wait_recv(blk, ("v", w, q))
+                for o in range(1, g.C):
+                    self._send(blk, blk, ("c", o, q, w), g.dev(c=o))
+
+    def step4(self):
+        g = self.g
+        U, V = g.size(self.u), g.size(self.v)
+        for q in range(U):
+            for w in range(V):
+                for o in range(1, g.C):
+                    self._wait_recv(self.block((U - q) % U, (V - w) % V, g.C - o), ("c", o, q, w))
+
+    def finish(self):
+        for cp in self.sent:
+            cp.wait_send()
+
+
+def run_gathers(gs):
+    n = len(gs)
+    for g in gs:
+        g.start()
+    steps = [lambda g: g.step1(), lambda g: g.step2(), lambda g: g.step3(), lambda g: g.step4()]
+    for t in range(n + 3):
+        for s in range(4):
+            i = t - s
+            if 0 <= i < n:
+                steps[s](gs[i])
+    for g in gs:
+        g.finish()
+
+class Scatter:
+    def __init__(self, grid, part, order, bufs, acc, out, ssem, rsem):
+        self.g, self.part, self.acc, self.out, self.ssem, self.rsem = grid, part, acc, out, ssem, rsem
+        self.rc, self.rv, self.ru, self.rz = bufs
+        self.u, self.v = order[1], order[2]
+        g = grid
+        U, V = g.size(self.u), g.size(self.v)
+        self.U, self.V = U, V
+        k = 0
+        self.slot = {}
+        for o in range(1, g.C):
+            for q in range(U):
+                for w in range(V):
+                    self.slot["c", o, q, w] = k; k += 1
+        for o in range(1, V):
+            for q in range(U):
+                self.slot["v", o, q] = k; k += 1
+        for o in range(1, U):
+            self.slot["u", o] = k; k += 1
+        for o in range(1, g.Z):
+            self.slot["z", o] = k; k += 1
+        self.sent = []
+
+    def first(self, uo, vo, co=0):
+        g = self.g.at(**{self.u: uo, self.v: vo, "c": co})
+        return self.g.dpof(g) * self.g.Z
+
+    def block(self, uo, vo, co=0):
+        return self.part.at[pl.ds(self.first(uo, vo, co), self.g.Z)]
+
+    def _copy(self, src, dst, slot, dev):
+        k = self.slot[slot]
+        return pltpu.make_async_remote_copy(src_ref=src, dst_ref=dst, send_sem=self.ssem.at[k], recv_sem=self.rsem.at[k],
+                                            device_id=dev, device_id_type=MESH)
+
+    def _send(self, src, dst, slot, dev):
+        cp = self._copy(src, dst, slot, dev)
+        cp.start()
+        self.sent.append((src, dst, slot, dev))
+
+    def _wait(self, dst, slot, dev):
+        self._copy(dst, dst, slot, dev).wait_recv()
+
+    def start(self):
+        g = self.g
+        for o in range(1, g.C):
+            for w in list(range(1, self.V)) + [0]:
+                for q in list(range(1, self.U)) + [0]:
+                    self._send(self.block(q, w, o), self.rc.at[o - 1, q * self.V + w], ("c", o, q, w), g.dev(c=o))
+
+    def step1(self):
+        g = self.g
+        f = jnp.float32
+        for w in list(range(1, self.V)) + [0]:
+            for q in list(range(1, self.U)) + [0]:
+                for o in range(1, g.C):
+                    self._wait(self.rc.at[o - 1, q * self.V + w], ("c", o, q, w), g.dev(c=o))
+                at = self.first(q, w)
+                def body(i, _):
+                    s = self.part[at + i].astype(f)
+                    for o in range(1, g.C):
+                        s = s + self.rc[o - 1, q * self.V + w, i].astype(f)
+                    if w:
+                        self.part[at + i] = s.astype(self.part.dtype)
+                    else:
+                        self.acc[q, i] = s
+                    return 0
+                lax.fori_loop(0, g.Z, body, 0)
+                if w:
+                    self._send(self.block(q, w), self.rv.at[w - 1, q], ("v", w, q), g.dev(**{self.v: w}))
+
+    def step2(self):
+        g = self.g
+        f = jnp.float32
+        for q in list(range(1, self.U)) + [0]:
+            for w in range(1, self.V):
+                self._wait(self.rv.at[w - 1, q], ("v", w, q), g.dev(**{self.v: w}))
+            at = self.first(q, 0)
+            def body(i, _):
+                s = self.acc[q, i]
+                for w in range(1, self.V):
+                    s = s + self.rv[w - 1, q, i].astype(f)
+                if q:
+                    self.part[at + i] = s.astype(self.part.dtype)
+                else:
+                    self.acc[q, i] = s
+                return 0
+            lax.fori_loop(0, g.Z, body, 0)
+            if q:
+                self._send(self.block(q, 0), self.ru.at[q - 1], ("u", q), g.dev(**{self.u: q}))
+
+    def step3(self):
+        g = self.g
+        f = jnp.float32
+        for q in range(1, self.U):
+            self._wait(self.ru.at[q - 1], ("u", q), g.dev(**{self.u: q}))
+        at = self.first(0, 0)
+        for o in list(range(1, g.Z)) + [0]:
+            i = (g.z + o) % g.Z
+            s = self.acc[0, i]
+            for q in range(1, self.U):
+                s = s + self.ru[q - 1, i].astype(f)
+            if o:
+                self.part[at + i] = s.astype(self.part.dtype)
+                self._send(self.part.at[at + i], self.rz.at[o - 1], ("z", o), g.dev(z=o))
+            else:
+                self.acc[0, i] = s
+
+    def step4(self):
+        g = self.g
+        s = self.acc[0, g.z]
+        for o in range(1, g.Z):
+            self._wait(self.rz.at[o - 1], ("z", o), g.dev(z=o))
+            s = s + self.rz[o - 1].astype(jnp.float32)
+        self.out[...] = s
+
+    def finish(self):
+        for a in self.sent:
+            self._copy(*a).wait_send()
+
+
+def scatter_scratch(grid_sizes, shape, dtype, order):
+    Z, S = grid_sizes["z"], grid_sizes
+    U, V, C = S[order[1]], S[order[2]], S["c"]
+    t = tuple(shape)
+    m = lambda n: max(n, 1)
+    return [pltpu.VMEM((m(C - 1), U * V, Z) + t, dtype), pltpu.VMEM((m(V - 1), U, Z) + t, dtype), pltpu.VMEM((m(U - 1), Z) + t, dtype),
+            pltpu.VMEM((m(Z - 1),) + t, dtype), pltpu.VMEM((U, Z) + t, jnp.float32)]
+
+
+def run_scatters(gs):
+    n = len(gs)
+    for g in gs:
+        g.start()
+    for t in range(n + 3):
+        for s in range(4):
+            i = t - s
+            if 0 <= i < n:
+                [gs[i].step1, gs[i].step2, gs[i].step3, gs[i].step4][s]()
+    for g in gs:
+        g.finish()
+
+
+ORDERS = ("zxyc", "zyxc", "zyxc", "zxyc", "zyxc", "zxyc")
+VMEM_CAP = 60 << 20
+
+
+def sizes_of(dp, seq):
+    C = 2 if dp % 2 == 0 else 1
+    rest = dp // C
+    y = 1
+    while (2 * y) * (2 * y) <= rest and rest % (2 * y) == 0:
+        y *= 2
+    return dict(y=y, x=rest // y, c=C, z=seq)
+
+
+def tiled(shard):
+    rows, cols = shard.shape
+    return shard.reshape((rows // 8, 8, cols) if rows % 8 == 0 else (1, rows, cols))
+
+
+def gather_kernel(dp, seq, orders, *refs):
+    n = len(orders)
+    ins, outs = refs[:n], refs[n : 2 * n]
+    ssem, rsem, lsem = refs[2 * n :]
+    grid = Grid(dp, seq)
+    entry_barrier(grid)
+    run_gathers(
+        [
+            Gather(grid, ins[i], outs[i], orders[i], ssem.at[i], rsem.at[i], lsem.at[i])
+            for i in range(n)
+        ]
+    )
+
+
+def gather_all(dp, seq, shards):
+    n = len(shards)
+    sems = pltpu.SemaphoreType.DMA((n, dp * seq - 1))
+    blocks = [tiled(s) for s in shards]
+    outs = pl.pallas_call(
+        partial(gather_kernel, dp, seq, ORDERS[:n]),
+        out_shape=[jax.ShapeDtypeStruct((dp * seq,) + b.shape, b.dtype) for b in blocks],
+        in_specs=[pl.BlockSpec(memory_space=pl.ANY)] * n,
+        out_specs=[pl.BlockSpec(memory_space=pl.ANY)] * n,
+        scratch_shapes=[sems, sems, pltpu.SemaphoreType.DMA((n,))],
+        compiler_params=pltpu.CompilerParams(collective_id=0, has_side_effects=True),
+        name="gather",
+    )(*blocks)
+    return [o.reshape((-1, s.shape[1])) for o, s in zip(outs, shards)]
+
+
+def scatter_kernel(dp, seq, orders, count, *refs):
+    n = len(orders)
+    ins, outs, total, rest = refs[:n], refs[n : 2 * n], refs[2 * n], refs[2 * n + 1 :]
+    parts, rest = rest[:n], rest[n:]
+    ssem, rsem, lsem, gs, gr = rest[-5:]
+    tail = rest[-6]
+    grid = Grid(dp, seq)
+    copies = [pltpu.make_async_copy(ins[i], parts[i], lsem.at[i]) for i in range(n)]
+    for c in copies:
+        c.start()
+    entry_barrier(grid)
+    for c in copies:
+        c.wait()
+    run_scatters(
+        [
+            Scatter(
+                grid, parts[i], orders[i], rest[5 * i : 5 * i + 4], rest[5 * i + 4], outs[i],
+                ssem.at[i], rsem.at[i],
+            )
+            for i in range(n)
+        ]
+    )
+    tail[...] = outs[n - 1][1:]
+    run_gathers([Gather(grid, tail, total, "zxyc", gs, gr, lsem.at[n])])
+
+
+def scatter_all(dp, seq, parts, orders):
+    n = len(parts)
+    N = dp * seq
+    sizes = sizes_of(dp, seq)
+    scratch = [pltpu.VMEM(p.shape, p.dtype) for p in parts]
+    for p, o in zip(parts, orders):
+        scratch += scatter_scratch(sizes, p.shape[1:], p.dtype, o)
+    last = parts[-1].shape[1:]
+    tail = (last[0] - 1,) + last[1:]
+    sems = pltpu.SemaphoreType.DMA((n, N - 1))
+    one = pltpu.SemaphoreType.DMA((N - 1,))
+    return pl.pallas_call(
+        partial(scatter_kernel, dp, seq, orders, n),
+        out_shape=[jax.ShapeDtypeStruct(p.shape[1:], jnp.float32) for p in parts]
+        + [jax.ShapeDtypeStruct((N,) + tail, jnp.float32)],
+        in_specs=[pl.BlockSpec(memory_space=pl.ANY)] * n,
+        out_specs=[pl.BlockSpec(memory_space=pltpu.VMEM)] * (n + 1),
+        scratch_shapes=scratch
+        + [
+            pltpu.VMEM(tail, jnp.float32), sems, sems, pltpu.SemaphoreType.DMA((n + 1,)), one, one,
+        ],
+        compiler_params=pltpu.CompilerParams(
+            collective_id=1, has_side_effects=True, vmem_limit_bytes=VMEM_CAP
+        ),
+        name="scatter",
+    )(*parts)
+
+
+def lanes(flat, rows):
+    return jnp.pad(flat, ((0, 0), (0, rows * 1024 - flat.shape[1]))).reshape(-1, rows, 8, 128)
+
+
+def cut(rows, widths):
+    out, at = [], 0
+    for w in widths:
+        out.append(rows[:, at : at + w])
+        at += w
+    return out
+
 
 HEADS = 6
 HEAD = 64
@@ -110,27 +525,18 @@
     hidden_units = FF
     ext_rows = local_rows + 2 * half_kernel
     score_scale = head_size ** (-0.5)
-    gathered = (
-        lax.all_gather(w_proj, ("dp", "seq"), axis=0, tiled=True),
-        lax.all_gather(w_depth, ("dp", "seq"), axis=0, tiled=True),
-        lax.all_gather(w_out, ("dp", "seq"), axis=0, tiled=True),
-        lax.all_gather(w_up, ("dp", "seq"), axis=0, tiled=True),
-        lax.all_gather(w_down, ("dp", "seq"), axis=0, tiled=True),
-        lax.all_gather(b_proj, ("dp", "seq"), axis=0, tiled=True),
-        lax.all_gather(b_up, ("dp", "seq"), axis=0, tiled=True),
-        lax.all_gather(b_out, ("dp", "seq"), axis=0, tiled=True),
-        lax.all_gather(ln1_gain, ("dp", "seq"), axis=0, tiled=True),
-        lax.all_gather(ln1_bias, ("dp", "seq"), axis=0, tiled=True),
-        lax.all_gather(b_down, ("dp", "seq"), axis=0, tiled=True),
-        lax.all_gather(ln2_gain, ("dp", "seq"), axis=0, tiled=True),
-        lax.all_gather(ln2_bias, ("dp", "seq"), axis=0, tiled=True),
-    )
+    dp, seq = lax.axis_size("dp"), lax.axis_size("seq")
+    devices = dp * seq
+    vectors = (b_proj, b_up, b_out, ln1_gain, ln1_bias, b_down, ln2_gain, ln2_bias)
+    widths = [w_depth.shape[0] * KERNEL] + [v.shape[0] for v in vectors]
+    small = jnp.concatenate([w_depth.reshape(-1)] + list(vectors))
+    small = jnp.pad(small, (0, 1024 - small.shape[0])).reshape(8, 128)
+    full_proj, full_out, full_up, full_down, small = gather_all(
+        dp, seq, [w_proj, w_out, w_up, w_down, small]
+    )
+    small = cut(small.reshape(devices, 1024), widths)
+    full_depth = small[0].reshape(-1, KERNEL)
     (
-        full_proj,
-        full_depth,
-        full_out,
-        full_up,
-        full_down,
         full_bproj,
         full_bup,
         full_bout,
@@ -139,7 +545,7 @@
         full_bdown,
         gain_two,
         shift_two,
-    ) = gathered
+    ) = [v.reshape(-1) for v in small[1:]]
     bias_proj = full_bproj.astype(jnp.float32)
     gain_first = gain_one.astype(jnp.float32)
     shift_first = shift_one.astype(jnp.float32)
@@ -248,30 +654,11 @@
     summed = summed + full_bdown.astype(jnp.float32) + first_norm
     out_value, second_pull = jax.vjp(layer_norm, summed, gain_second, shift_second)
     output = out_value.astype(jnp.bfloat16).reshape(seq_count, local_rows, model_width)
-    back_set = (
-        lax.all_gather(w_proj, ("dp", "seq"), axis=0, tiled=True),
-        lax.all_gather(w_depth, ("dp", "seq"), axis=0, tiled=True),
-        lax.all_gather(w_out, ("dp", "seq"), axis=0, tiled=True),
-        lax.all_gather(w_up, ("dp", "seq"), axis=0, tiled=True),
-        lax.all_gather(w_down, ("dp", "seq"), axis=0, tiled=True),
-        lax.all_gather(b_proj, ("dp", "seq"), axis=0, tiled=True),
-        lax.all_gather(b_up, ("dp", "seq"), axis=0, tiled=True),
-        lax.all_gather(b_out, ("dp", "seq"), axis=0, tiled=True),
-        lax.all_gather(ln1_gain, ("dp", "seq"), axis=0, tiled=True),
-        lax.all_gather(ln1_bias, ("dp", "seq"), axis=0, tiled=True),
-        lax.all_gather(b_down, ("dp", "seq"), axis=0, tiled=True),
-        lax.all_gather(ln2_gain, ("dp", "seq"), axis=0, tiled=True),
-        lax.all_gather(ln2_bias, ("dp", "seq"), axis=0, tiled=True),
-    )
-    back_proj = back_set[0]
-    back_depth = back_set[1].astype(jnp.float32)
-    back_out = back_set[2]
-    back_up = back_set[3].reshape(
-        group_count, model_width // group_count, hidden_units // group_count
-    )
-    back_down = back_set[4].reshape(
-        group_count, hidden_units // group_count, model_width // group_count
-    )
+    back_proj = full_proj
+    back_depth = full_depth.astype(jnp.float32)
+    back_out = full_out
+    back_up = up_groups
+    back_down = down_groups
     grad_summed, grad_gain_two, grad_shift_two = second_pull(
         cotangent.reshape(total_rows, model_width).astype(jnp.float32)
     )
@@ -409,22 +796,47 @@
             grad_bpt,
         ]
     )
-    shards = (
-        lax.psum_scatter(grad_wproj, ("dp", "seq"), scatter_dimension=0, tiled=True),
-        lax.psum_scatter(grad_wdepth, ("dp", "seq"), scatter_dimension=0, tiled=True),
-        lax.psum_scatter(grad_wout, ("dp", "seq"), scatter_dimension=0, tiled=True),
-        lax.psum_scatter(grad_wup, ("dp", "seq"), scatter_dimension=0, tiled=True),
-        lax.psum_scatter(grad_wdown, ("dp", "seq"), scatter_dimension=0, tiled=True),
-        lax.psum_scatter(grad_bproj, ("dp", "seq"), scatter_dimension=0, tiled=True),
-        lax.psum_scatter(grad_bup, ("dp", "seq"), scatter_dimension=0, tiled=True),
-        lax.psum_scatter(grad_bout, ("dp", "seq"), scatter_dimension=0, tiled=True),
-        lax.psum_scatter(grad_gain_one, ("dp", "seq"), scatter_dimension=0, tiled=True),
-        lax.psum_scatter(grad_shift_one, ("dp", "seq"), scatter_dimension=0, tiled=True),
-        lax.psum_scatter(grad_bdown, ("dp", "seq"), scatter_dimension=0, tiled=True),
-        lax.psum_scatter(grad_gain_two, ("dp", "seq"), scatter_dimension=0, tiled=True),
-        lax.psum_scatter(grad_shift_two, ("dp", "seq"), scatter_dimension=0, tiled=True),
-    )
-    kernel_total = lax.psum((grad_wkernel, grad_bkernel), ("dp", "seq"))
+    def blocks(grad, shard):
+        return grad.astype(jnp.bfloat16).reshape((devices,) + tiled(shard).shape)
+
+    per_device = [
+        g.reshape(devices, -1)
+        for g in (
+            grad_wdepth, grad_bproj, grad_bup, grad_bout, grad_gain_one, grad_shift_one,
+            grad_bdown, grad_gain_two, grad_shift_two,
+        )
+    ]
+    kernel_flat = jnp.concatenate([grad_wkernel.reshape(-1), grad_bkernel])
+    kernel_len = kernel_flat.shape[0]
+    kernel_each = -(-kernel_len // devices)
+    kernel_flat = jnp.pad(kernel_flat, (0, kernel_each * devices - kernel_len))
+    small_grad = jnp.concatenate(
+        [
+            lanes(jnp.concatenate(per_device, axis=1), 1),
+            lanes(kernel_flat.reshape(devices, kernel_each), 1),
+        ],
+        axis=1,
+    )
+    sum_down, sum_up, sum_out, sum_proj, sum_small, sum_kernel = scatter_all(
+        dp,
+        seq,
+        [
+            blocks(grad_wdown, w_down), blocks(grad_wup, w_up), blocks(grad_wout, w_out),
+            blocks(grad_wproj, w_proj), small_grad,
+        ],
+        ("zxyc", "zyxc", "zxyc", "zyxc", "zxyc"),
+    )
+    mine = cut(sum_small[:1].reshape(1, 1024), widths)
+    shards = [sum_proj.reshape(w_proj.shape), mine[0].reshape(w_depth.shape)]
+    shards += [
+        sum_out.reshape(w_out.shape), sum_up.reshape(w_up.shape), sum_down.reshape(w_down.shape),
+    ]
+    shards += [m.reshape(-1) for m in mine[1:]]
+    kernel_sum = sum_kernel.reshape(devices, 1024)[:, :kernel_each].reshape(-1)
+    kernel_total = (
+        kernel_sum[: grad_wkernel.size].reshape(grad_wkernel.shape),
+        kernel_sum[grad_wkernel.size : kernel_len],
+    )
     return (
         output,
         grad_tokens.reshape(seq_count, local_rows, model_width),

time: 986 us -> 444 us (0.45)
  waiting for transfers between devices: 580 us -> 42.9 us
  blocking collectives: 152 us -> 0 us
  Pallas kernels: 0 us -> 135 us
  local copies, waits for them, and re-layouts: 64.8 us -> 80.3 us
  matrix products: 97.8 us -> 87.4 us
    reduce_scatter x3 -> x0, waiting for transfers between devices: 328 us -> none  [the longest x1 113 us: body(): lax.psum_scatter(grad_wup, ('dp', 'seq'), scatter_dimension=0, tiled=True)]
    pallas_call x0 -> x2, Pallas kernels: none -> 135 us  [the longest x1 77.3 us: scatter_all(): pl.pallas_call(partial(scatter_kernel, dp, seq, orders, n), out_shape=[ja...]
    all_gather x4 -> x0, waiting for transfers between devices: 132 us -> none  [the longest x1 52.4 us: body(): lax.all_gather(w_up, ('dp', 'seq'), axis=0, tiled=True)]
    unnamed x2 -> x0, blocking collectives: 85.1 us -> none
    unnamed x12 -> x3, waiting for transfers between devices: 80.3 us -> 0.05 us
    all_gather x1 -> x0, blocking collectives: 66.9 us -> none  [body(): lax.all_gather(w_depth, ('dp', 'seq'), axis=0, tiled=True)]
    all_gather x1, waiting for transfers between devices: 0.01 us -> 38.5 us  [body(): lax.all_gather(key_rows.reshape(seq_count, local_rows, all_width), 'seq',...]
    reduce_scatter x1, waiting for transfers between devices: 36.2 us -> 0.01 us  [body(): lax.psum_scatter(kv_terms.astype(jnp.bfloat16), 'seq', scatter_dimension=...]
  transfers between devices with their start and end apart: 15 -> 7, of which waited for: 10 -> 2; matrix products, arithmetic and copies ran while one was open for 11% -> 18% of each run, Pallas kernels for 0% -> 0%
where the time goes in v1:
time: 444 us; the launch traced here: 438 us
  Pallas kernels  135 us (30%)
  matrix products  87.4 us (20%)
  local copies, waits for them, and re-layouts  80.3 us (18%)
  other arithmetic  62.9 us (14%)
  waiting for transfers between devices  42.9 us (10%)
  between operations  15.6 us (4%)
  starting transfers between devices  13.6 us (3%)
    pallas_call x1, Pallas kernels, scatter_all(): pl.pallas_call(partial(scatter_kernel, dp, seq, orders, n), out_shape=[ja...  77.3 us
    pallas_call x1, Pallas kernels, gather_all(): pl.pallas_call(partial(gather_kernel, dp, seq, ORDERS[:n]), out_shape=[ja...  57.4 us
    all_gather x1, waiting for transfers between devices, body(): lax.all_gather(key_rows.reshape(seq_count, local_rows, all_width), 'seq',...  38.5 us
    unnamed x203, local copies, waits for them, and re-layouts  22.4 us
    dot_general x1, matrix products, body(): jnp.einsum('ngd,gdf->ngf', grouped_in, up_groups, preferred_element_type=...  16.1 us
    add x1, other arithmetic, body(): grad_conv_ext + jnp.pad(tap_weights[..., tap_index, None] * grad_mix, ((0...  11.6 us
    reduce_sum x1, other arithmetic, body(): jnp.sum(grad_mix * conv_heads[:, tap_index:tap_index + local_rows], axis=-1)  11.2 us
    ppermute x2, starting transfers between devices, with_halo(): lax.ppermute(tail, axis, [(i, (i + 1) % count) for i in range(ends)])  10.9 us
  transfers between devices with their start and end apart: 7, of which 2 were waited for; matrix products, arithmetic and copies ran while one was open for 18% of the time, Pallas kernels for 0%

profile of v1, /device:TPU:0, one launch (start us, length us, event | category | flops | bytes accessed | tf_op | source)
XLA Modules:
  0.0 438.2 jit_solution(6188153304832676271)
XLA Ops:
  8.1 5.4 %concatenate.65 = bf16[504]{0:T(512)(128)(2,1)S(1)} concatenate(bf16[216]{0:T(256)(128)(2,1)S(1)} %reshape.550, bf16[48]{0:T(256)(128)(2,1)} %param.34, bf16[96]{0:T(256)(128)(2,1)} %param.35, bf16[24]{0:T(256)(128)(2,1)} %param.36, bf16[24]{0:T(256)(128)(2,1)} %param.37, bf16[24]{0:T(256)(128)(2,1)} %param.38, bf16[24]{0:T(256)(128)(2,1)} %param.39, bf16[24]{0:T(256)(128)(2,1)} %param.40, ...), dimensions={0} | concatenate | bytes 2016 | tf_op jit(solution)/shard_map/concatenate | solution.py:532
  14.2 57.4 %gather.1 = (bf16[32,3,8,1920]{3,2,1,0:T(8,128)(2,1)}, bf16[32,3,8,768]{3,2,1,0:T(8,128)(2,1)}, bf16[32,3,8,1536]{3,2,1,0:T(8,128)(2,1)}, bf16[32,12,8,384]{3,2,1,0:T(8,128)(2,1)}, bf16[32,1,8,128]{3,2,1,0:T(8,128)(2,1)}) custom-call(bf16[3,8,1920]{2,1,0:T(8,128)(2,1)} %bitcast.465, bf16[3,8,768]{2,1,0:T(8,128)(2,1)} %bitcast.470, ...), custom_call_target="tpu_custom_call" | custom-call | tf_op jit(solution)/shard_map/gather/pallas_call | solution.py:345
  72.7 2.9 convolution_bitcast_fusion
  79.6 8.2 %collective-permute-start = (bf16[2,4,768]{2,1,0:T(4,128)(2,1)S(1)}, bf16[2,4,768]{2,1,0:T(4,128)(2,1)S(1)}, u32[]{:S(2)}, u32[]{:S(2)}) collective-permute-start(bf16[2,4,768]{2,1,0:T(4,128)(2,1)S(1)} %get-tuple-element.304), channel_id=1, source_target_pairs={{0,1},{1,2},{2,3},{4,5},{5,6},{6,7},{8,9},{9,10},{10,11},{12,13},{... | collective-permute-start | bytes 36872 | tf_op jit(solution)/shard_map/ppermute | solution.py:441
  105.6 6.7 %add_convert_fusion.3 = bf16[2,256,6,64]{1,0,3,2:T(2,128)(2,1)S(1)} fusion(f32[2,264,6,64]{1,0,3,2:T(2,128)S(1)} %broadcast_multiply_fusion.9, f32[2,256,6]{1,0,2:T(2,128)S(1)} %get-tuple-element.307, f32[2,256,6]{1,0,2:T(2,128)S(1)} %get-tuple-element.308, f32[2,256,6]{1,0,2:T(2,128)S(1)} %get-tuple-element.309, f32[2,256,6]{1,0,2:T(2,128)S(1)} %get-tuple-element.310, ...), kind=kLoop, calls=%fused_computation.184 | loop fusion | flops 3538944 | bytes 7581696 | tf_op jit(solution)/shard_map/convert_element_type | solution.py:625
  115.1 4.4 %all-gather.3.cloned.1.call-done = bf16[2,1024,384]{1,2,0:T(8,128)(2,1)} async-done(((bf16[2,256,384]{1,2,0:T(8,128)(2,1)}), bf16[2,1024,384]{1,2,0:T(8,128)(2,1)}) %all-gather.3.cloned.1.call-update) | async-done | bytes 1572880 | tf_op jit(solution)/shard_map/all_gather | solution.py:606
  119.5 38.5 %all-gather.5.cloned.1.call-done = bf16[2,1024,384]{1,2,0:T(8,128)(2,1)} async-done(((bf16[2,256,384]{1,2,0:T(8,128)(2,1)}), bf16[2,1024,384]{1,2,0:T(8,128)(2,1)}) %all-gather.5.cloned.1.call-update) | async-done | bytes 1572880 | tf_op jit(solution)/shard_map/all_gather | solution.py:603
  158.0 12.2 %while.26 = (s32[]{:T(128)}, bf16[2,256,6,64]{1,3,2,0:T(8,128)(2,1)}, f32[2,6,256]{2,1,0:T(8,128)S(1)}, bf16[2,1024,384]{1,2,0:T(8,128)(2,1)}, bf16[2,256,384]{1...) while((s32[]{:T(128)}, bf16[2,256,6,64]{1,3,2,0:T(8,128)(2,1)}, f32[2,6,256]{2,1,0:T(8,128)S(1)}, ...), condition=%wide.region_3.4_spmd, body=%wide.region_0.3_spmd.sunk | while | flops 415332864 | bytes 27584660 | solution.py:621
  174.7 16.1 %fusion.22 = (bf16[512,2,1536]{2,0,1:T(8,128)(2,1)S(1)}, f32[512,2,1536]{2,0,1:T(8,128)}, f32[2,1536,512]{1,2,0:T(8,128)}) fusion(f32[2,1536]{1,0:T(2,128)S(1)} %reshape.608, bf16[2,384,1536]{2,1,0:T(8,128)(2,1)S(1)} %bitcast.480, bf16[64,2,8,384]{3,2,1,0:T(8,128)(2,1)S(1)} %bitcast.434), kind=kOutput, calls=%fused_computation.49 | convolution fusion | flops 1311768576 | bytes 18886656 | tf_op jit(solution)/shard_map/ngd,gdf->ngf/dot_general | solution.py:641
  193.7 3.1 copy.91
  204.7 7.1 %fusion.125 = (f32[2,1536]{1,0:T(2,128)}, bf16[512,2,1536]{2,0,1:T(8,128)(2,1)S(1)}) fusion(f32[512,2,1536]{2,0,1:T(8,128)S(1)} %copy-done.91, bf16[2,1536,384]{2,1,0:T(8,128)(2,1)S(1)} %bitcast.483, bf16[64,2,8,384]{3,2,1,0:T(8,128)(2,1)S(1)} %bitcast.436, f32[2,1536,512]{1,2,0:T(8,128)} %get-tuple-element.333, f32[2,1536]{1,0:T(2,128)S(1)} %reshape.608), kind=kOutput, calls=%fused_computation.319 | convolution fusion | flops 1233122304 | bytes 18898944 | tf_op jit(solution)/shard_map/ngd,gfd->ngf/dot_general | solution.py:669
  214.3 3.0 copy.92
  217.3 3.3 multiply_reduce_fusion.2
  225.7 11.2 %multiply_reduce_fusion.6 = (f32[2,256,6]{1,0,2:T(2,128)S(1)}, f32[2,256,6]{1,0,2:T(2,128)S(1)}, f32[2,256,6]{1,0,2:T(2,128)S(1)}, f32[2,256,6]{1,0,2:T(2,128)S(...) fusion(f32[2,256,6,64]{1,0,3,2:T(2,128)S(1)} %reshape.569, ...), kind=kLoop, calls=%fused_computation.175 | loop fusion | flops 5280768 | bytes 15163392 | tf_op jit(solution)/shard_map/reduce_sum | solution.py:723
  237.1 34.8 %while.27 = (s32[]{:T(128)}, f32[2,256,384]{2,1,0:T(8,128)}, bf16[2,1024,768]{1,2,0:T(8,128)(2,1)}, bf16[2,1024,384]{1,2,0:T(8,128)(2,1)}, bf16[2,256,384]{1,2,0...) while((s32[]{:T(128)}, f32[2,256,384]{2,1,0:T(8,128)}, ...), condition=%wide.region_16.17_spmd, body=%wide.region_14.16_spmd.sunk | while | flops 1029536256 | bytes 111716632 | solution.py:713
  238.8 3.7 fusion.192
  242.7 4.5 %multiply_reduce_fusion.19 = (f32[6,256]{1,0:T(8,128)S(1)}, f32[6,256,1024]{2,1,0:T(8,128)S(1)}) fusion(f32[6,256,1024]{2,1,0:T(8,128)} %fusion.192, f32[6,256]{1,0:T(8,128)S(1)} %dynamic-slice_bitcast_fusion.2, bf16[256,6,64]{0,2,1:T(8,128)(2,1)S(1)} %bitcast.406, bf16[1024,6,64]{0,2,1:T(8,128)(2,1)S(1)} %bitcast.399), kind=kOutput, calls=%fused_computation.16.clone.1 | convolution fusion | flops 207616512 | bytes 13578240 | tf_op jit(solution)/shard_map/while/body/eval_jaxpr/ihe,jhe->hij/dot_general | solution.py:476
  256.1 3.7 fusion.192
  260.0 4.5 %multiply_reduce_fusion.19 = (f32[6,256]{1,0:T(8,128)S(1)}, f32[6,256,1024]{2,1,0:T(8,128)S(1)}) fusion(f32[6,256,1024]{2,1,0:T(8,128)} %fusion.192, f32[6,256]{1,0:T(8,128)S(1)} %dynamic-slice_bitcast_fusion.2, bf16[256,6,64]{0,2,1:T(8,128)(2,1)S(1)} %bitcast.406, bf16[1024,6,64]{0,2,1:T(8,128)(2,1)S(1)} %bitcast.399), kind=kOutput, calls=%fused_computation.16.clone.1 | convolution fusion | flops 207616512 | bytes 13578240 | tf_op jit(solution)/shard_map/while/body/eval_jaxpr/ihe,jhe->hij/dot_general | solution.py:476
  273.3 11.6 %pad_add_fusion.1 = f32[2,264,6,64]{1,0,3,2:T(2,128)S(1)} fusion(f32[2,256,6,64]{1,0,3,2:T(2,128)} %get-tuple-element.303, f32[2,256,6,64]{1,0,3,2:T(2,128)} %get-tuple-element.302, f32[2,256,6,64]{1,0,3,2:T(2,128)} %get-tuple-element.301, f32[2,256,6,64]{1,0,3,2:T(2,128)} %get-tuple-element.300, f32[2,256,6,64]{1,0,3,2:T(2,128)} %get-tuple-element.299, ...), kind=kLoop, calls=%fused_computation.150 | loop fusion | flops 1622016 | bytes 7888896 | tf_op jit(solution)/shard_map/add | solution.py:730
  288.8 4.4 %fusion.57 = (f32[768]{0:T(1024)S(1)}, f32[768]{0:T(1024)S(1)}, f32[768]{0:T(1024)S(1)}, f32[768]{0:T(1024)S(1)}, f32[768]{0:T(1024)S(1)}, /*index=5*/f32[768]{0...) fusion(bf16[2,260,768]{2,1,0:T(8,128)(2,1)S(1)} %copy-done.2, ...), kind=kOutput, calls=%fused_computation.116 | convolution fusion | flops 317908224 | bytes 7314432 | tf_op jit(solution)/shard_map/dot_general | solution.py:749
  314.2 3.3 convolution_convert_fusion.1
  340.8 77.3 %scatter.1 = (f32[12,8,384]{2,1,0:T(8,128)}, f32[3,8,1536]{2,1,0:T(8,128)}, f32[3,8,768]{2,1,0:T(8,128)}, f32[3,8,1920]{2,1,0:T(8,128)}, f32[2,8,128]{2,1,0:T(8,128)}, /*index=5*/f32[32,1,8,128]{3,2,1,0:T(8,128)}) custom-call(bf16[32,12,8,384]{3,2,1,0:T(8,128)(2,1)} %bitcast.420, bf16[32,3,8,1536]{3,2,1,0:T(8,128)(2,1)} %bitcast.419, ...), custom_call_target="tpu_custom_call" | custom-call | tf_op jit(solution)/shard_map/scatter/pallas_call | solution.py:394
  424.0 4.8 %bitcast_add_fusion = f32[512,768]{1,0:T(8,128)} fusion(f32[2,256,768]{2,1,0:T(8,128)S(1)} %copy-done.30, bf16[768,1920]{1,0:T(8,128)(2,1)} %bitcast.479, f32[512,768]{1,0:T(8,128)S(1)} %copy-done.18, f32[512]{0:T(512)S(1)} %copy-done.78, bf16[512,384]{1,0:T(8,128)(2,1)} %bitcast.450, bf16[512,384]{1,0:T(8,128)(2,1)} %bitcast.455, ...), kind=kOutput, calls=%fused_computation.118 | convolution fusion | flops 1215430656 | bytes 8652800 | tf_op jit(solution)/shard_map/dot_general | solution.py:787
  (429 shorter events, 136.7 us)
Async XLA Ops:
  7.2 91.9 %copy-start = (bf16[384,54]{0,1:T(8,128)(2,1)S(1)}, bf16[384,54]{0,1:T(8,128)(2,1)}, u32[]{:S(2)}) copy-start(bf16[384,54]{0,1:T(8,128)(2,1)} %param.29) | copy-start | bytes 124420
  7.2 112.3 %all-gather.3.cloned.1.call-start = ((), (), s32[]{:S(2)}) async-start(), calls=%async_computation.1 | async-start | bytes 1966080 | tf_op jit(solution)/shard_map/all_gather | solution.py:606
  77.2 21.9 %copy-start.3 = (bf16[512,384]{1,0:T(8,128)(2,1)}, bf16[512,384]{1,0:T(8,128)(2,1)S(1)}, u32[]{:S(2)}) copy-start(bf16[512,384]{1,0:T(8,128)(2,1)S(1)} %get-tuple-element.276) | copy-start | bytes 1179652
  78.2 79.8 %all-gather.5.cloned.1.call-start = ((), (), s32[]{:S(2)}) async-start(), calls=%async_computation.2 | async-start | bytes 1966080 | tf_op jit(solution)/shard_map/all_gather | solution.py:603
  78.3 15.9 %collective-permute-start.1 = (bf16[2,4,768]{2,1,0:T(4,128)(2,1)S(1)}, bf16[2,4,768]{2,1,0:T(4,128)(2,1)S(1)}, u32[]{:S(2)}, u32[]{:S(2)}) collective-permute-start(bf16[2,4,768]{2,1,0:T(4,128)(2,1)S(1)} %get-tuple-element.305), channel_id=1, source_target_pairs={{1,0},{2,1},{3,2},{5,4},{6,5},{7,6},{9,8},{10,9},{11,10},{13,12},{... | collective-permute-start | bytes 36872 | tf_op jit(solution)/shard_map/ppermute | solution.py:443
  79.6 14.7 %collective-permute-start = (bf16[2,4,768]{2,1,0:T(4,128)(2,1)S(1)}, bf16[2,4,768]{2,1,0:T(4,128)(2,1)S(1)}, u32[]{:S(2)}, u32[]{:S(2)}) collective-permute-start(bf16[2,4,768]{2,1,0:T(4,128)(2,1)S(1)} %get-tuple-element.304), channel_id=1, source_target_pairs={{0,1},{1,2},{2,3},{4,5},{5,6},{6,7},{8,9},{9,10},{10,11},{12,13},{... | collective-permute-start | bytes 36872 | tf_op jit(solution)/shard_map/ppermute | solution.py:441
  90.0 243.6 %reduce-scatter.2.cloned.1.call-start = ((), (), s32[]{:S(2)}) async-start(), calls=%async_computation.3 | async-start | bytes 3932160 | tf_op jit(solution)/shard_map/reduce_scatter | solution.py:716
  173.6 17.2 %copy-start.33 = (bf16[512,768]{1,0:T(8,128)(2,1)}, bf16[512,768]{1,0:T(8,128)(2,1)S(1)}, u32[]{:S(2)}) copy-start(bf16[512,768]{1,0:T(8,128)(2,1)S(1)} %fusion.67) | copy-start | bytes 2359300
  174.7 16.1 %copy-start.82 = (bf16[32,12,8,384]{3,2,1,0:T(8,128)(2,1)S(1)}, bf16[32,12,8,384]{3,2,1,0:T(8,128)(2,1)}, u32[]{:S(2)}) copy-start(bf16[32,12,8,384]{3,2,1,0:T(8,128)(2,1)} %get-tuple-element.128) | copy-start | bytes 7077892
  204.2 7.5 %copy-start.37 = (bf16[512,768]{1,0:T(8,128)(2,1)}, bf16[512,768]{1,0:T(8,128)(2,1)S(1)}, u32[]{:S(2)}) copy-start(bf16[512,768]{1,0:T(8,128)(2,1)S(1)} %get-tuple-element.280) | copy-start | bytes 2359300
  204.7 7.1 %copy-start.81 = (bf16[32,3,8,1536]{3,2,1,0:T(8,128)(2,1)S(1)}, bf16[32,3,8,1536]{3,2,1,0:T(8,128)(2,1)}, u32[]{:S(2)}) copy-start(bf16[32,3,8,1536]{3,2,1,0:T(8,128)(2,1)} %get-tuple-element.129) | copy-start | bytes 7077892
  221.3 84.3 %copy-start.77 = (f32[512]{0:T(512)}, f32[512]{0:T(512)S(1)}, u32[]{:S(2)}) copy-start(f32[512]{0:T(512)S(1)} %negate_multiply_fusion.1) | copy-start | bytes 6148
  296.0 5.9 %copy-start.15 = (f32[512,384]{1,0:T(8,128)S(1)}, f32[512,384]{1,0:T(8,128)}, u32[]{:S(2)}) copy-start(f32[512,384]{1,0:T(8,128)} %copy-done.14) | copy-start | bytes 2359300
  297.8 27.1 %collective-permute-start.2 = (bf16[2,4,1152]{2,1,0:T(4,128)(2,1)}, bf16[2,4,1152]{2,1,0:T(4,128)(2,1)S(1)}, u32[]{:S(2)}, u32[]{:S(2)}) collective-permute-start(bf16[2,4,1152]{2,1,0:T(4,128)(2,1)} %get-tuple-element.290), channel_id=1, source_target_pairs={{0,1},{1,2},{2,3},{4,5},{5,6},{6,7},{8,9},{9,10},{10,11},{12,13},{... | collective-permute-start | bytes 55304 | tf_op jit(solution)/shard_map/ppermute | solution.py:441
  300.5 24.4 %collective-permute-start.3 = (bf16[2,4,1152]{2,1,0:T(4,128)(2,1)}, bf16[2,4,1152]{2,1,0:T(4,128)(2,1)S(1)}, u32[]{:S(2)}, u32[]{:S(2)}) collective-permute-start(bf16[2,4,1152]{2,1,0:T(4,128)(2,1)} %get-tuple-element.291), channel_id=1, source_target_pairs={{1,0},{2,1},{3,2},{5,4},{6,5},{7,6},{9,8},{10,9},{11,10},{13,12},{... | collective-permute-start | bytes 55304 | tf_op jit(solution)/shard_map/ppermute | solution.py:443
  314.2 6.0 %copy-start.79 = (f32[768]{0:T(1024)S(1)}, f32[768]{0:T(1024)}, u32[]{:S(2)}) copy-start(f32[768]{0:T(1024)} %get-tuple-element.214) | copy-start | bytes 9220
  329.6 5.4 %copy-start.53 = (f32[32,24]{1,0:T(8,128)S(1)}, f32[32,24]{1,0:T(8,128)}, u32[]{:S(2)}) copy-start(f32[32,24]{1,0:T(8,128)} %reshape.582) | copy-start | bytes 9220
  329.6 5.4 %copy-start.54 = (f32[32,24]{1,0:T(8,128)S(1)}, f32[32,24]{1,0:T(8,128)}, u32[]{:S(2)}) copy-start(f32[32,24]{1,0:T(8,128)} %reshape.577) | copy-start | bytes 9220
  340.8 83.2 %copy-start.18 = (f32[512,768]{1,0:T(8,128)S(1)}, f32[512,768]{1,0:T(8,128)}, u32[]{:S(2)}) copy-start(f32[512,768]{1,0:T(8,128)} %copy-done.16) | copy-start | bytes 4718596
  340.8 83.2 %copy-start.30 = (f32[2,256,768]{2,1,0:T(8,128)S(1)}, f32[2,256,768]{2,1,0:T(8,128)}, u32[]{:S(2)}) copy-start(f32[2,256,768]{2,1,0:T(8,128)} %slice.508) | copy-start | bytes 4718596
  340.8 83.2 %copy-start.78 = (f32[512]{0:T(512)S(1)}, f32[512]{0:T(512)}, u32[]{:S(2)}) copy-start(f32[512]{0:T(512)} %copy-done.77) | copy-start | bytes 6148
  423.9 5.5 %copy-start.52 = (f32[3,8,768]{2,1,0:T(8,128)S(1)}, f32[3,8,768]{2,1,0:T(8,128)}, u32[]{:S(2)}) copy-start(f32[3,8,768]{2,1,0:T(8,128)} %get-tuple-element.140) | copy-start | bytes 221188
  424.0 6.2 %copy-start.51 = (f32[3,8,1536]{2,1,0:T(8,128)S(1)}, f32[3,8,1536]{2,1,0:T(8,128)}, u32[]{:S(2)}) copy-start(f32[3,8,1536]{2,1,0:T(8,128)} %get-tuple-element.141) | copy-start | bytes 442372
  424.0 6.8 %copy-start.50 = (f32[12,8,384]{2,1,0:T(8,128)S(1)}, f32[12,8,384]{2,1,0:T(8,128)}, u32[]{:S(2)}) copy-start(f32[12,8,384]{2,1,0:T(8,128)} %get-tuple-element.142) | copy-start | bytes 442372
  (85 other events, 225.4 us)
Sparse Core Ops, SparseCore 0:
  78.3 41.1 all-gather.2
  121.0 36.8 all-gather.4
  272.0 58.8 reduce-scatter.1
